TPU v7x, 32 devices: a whole 2x2x4 slice. The times are simulated.
32 devices in a mesh: row: 4 (over z), col: 8 (over y, x, core).
Axes of the slice: x: 2, y: 2, z: 4, core: 2. Of those that a mesh axis runs over, the one named last changes fastest.
Arguments:
- occupations: int32 [4096, 128], P('row'), may hold values from 0 to 2
- table: float32 [384, 1024], replicated, may hold values from -0.5 to 0.5
- weights: float32 [2, 1024, 4096], P(None, None, 'col'), may hold values from -0.1875 to 0.1875
- biases: float32 [2, 4096], P(None, 'col'), may hold values from -6 to 6
- heads: float32 [2, 4096], P(None, 'col'), may hold values from -18 to 18
- energies: float32 [4096], P('row'), may hold values from -6 to 6
Outputs:
- schur: float32 [4096, 4096], P('row', 'col')
- solved_rhs: float32 [4096], P('row')
All inputs are finite; a program needn't handle non-finite values.
Results may differ from a plain program's by a relative error of at most 0.0034.
Values may be sent and summed in bfloat16 or wider, within the bound.
A program may use at most 128 MiB of HBM per device.

v0:
```python
import math
import jax
import jax.numpy as jnp
from jax import lax
from jax.sharding import PartitionSpec as P

norm_eps = 1e-06
diag_shift = 0.05


def broadcast(block, axis, holder):
    block = jnp.where(lax.axis_index(axis) == holder, block, jnp.zeros_like(block))
    return lax.psum(block, axis)


def jacobian(occupations, table, weights, biases, heads):
    onehot = jnp.concatenate(
        [
            (occupations == 0).astype(jnp.float32),
            (occupations == 1).astype(jnp.float32),
            (occupations == 2).astype(jnp.float32),
        ],
        axis=1,
    )
    embedded = jnp.dot(
        onehot, table, precision=lax.Precision.HIGHEST, preferred_element_type=jnp.float32
    )
    embedded = embedded * lax.rsqrt(
        jnp.mean(embedded * embedded, axis=-1, keepdims=True) + norm_eps
    )
    blocks = []
    for panel_index in range(2):
        hidden = (
            jnp.dot(
                embedded,
                weights[panel_index],
                precision=lax.Precision.HIGHEST,
                preferred_element_type=jnp.float32,
            )
            + biases[panel_index]
        )
        blocks.append(heads[panel_index] * jax.nn.sigmoid(hidden))
    return jnp.concatenate(blocks, axis=1)


def on_device(occupations, table, weights, biases, heads, energies):
    row_count = occupations.shape[0]
    row_devices = lax.axis_size("row")
    col_devices = lax.axis_size("col")
    sample_total = row_count * row_devices
    panel_width = sample_total // col_devices
    derivs = jacobian(occupations, table, weights, biases, heads)
    col_sums = lax.psum(jnp.sum(derivs, axis=0), "row")
    centered = ((derivs - col_sums / sample_total) * (1.0 / math.sqrt(sample_total))).astype(
        jnp.bfloat16
    )
    own_rows = lax.all_gather(centered, "col", axis=1, tiled=True)
    every_sample = lax.all_gather(centered, "row", axis=0, tiled=True)
    partner = lax.all_to_all(every_sample, "col", split_axis=0, concat_axis=1, tiled=True)
    kernel = lax.dot_general(
        own_rows, partner, (((1,), (1,)), ((), ())), preferred_element_type=jnp.float32
    )
    row_ids = lax.axis_index("row") * row_count + lax.iota(jnp.int32, row_count)
    col_ids = lax.axis_index("col") * panel_width + lax.iota(jnp.int32, panel_width)
    kernel = kernel + jnp.where(row_ids[:, None] == col_ids[None, :], diag_shift, 0.0).astype(
        jnp.float32
    )
    right_side = energies
    for panel_index in range(2):
        start_global = panel_index * panel_width
        root_row = start_global // row_count
        offset = start_global % row_count
        top_block, top_side = (
            broadcast(kernel[offset : offset + panel_width], "row", root_row),
            broadcast(right_side[offset : offset + panel_width], "row", root_row),
        )
        column, diag_block = (
            broadcast(kernel, "col", panel_index),
            broadcast(top_block, "col", panel_index),
        )
        factor = jnp.linalg.cholesky(diag_block)
        left_rows = lax.linalg.triangular_solve(
            factor, column, left_side=False, lower=True, transpose_a=True
        )
        right_rows = lax.linalg.triangular_solve(
            factor, top_block.T, left_side=False, lower=True, transpose_a=True
        )
        kernel = kernel - lax.dot_general(
            left_rows,
            right_rows,
            (((1,), (1,)), ((), ())),
            precision=lax.Precision.HIGHEST,
            preferred_element_type=jnp.float32,
        )
        solved = lax.linalg.triangular_solve(factor, top_side[:, None], left_side=True, lower=True)[
            :, 0
        ]
        right_side = right_side - jnp.dot(
            left_rows, solved, precision=lax.Precision.HIGHEST, preferred_element_type=jnp.float32
        )
        placed = right_side.at[offset : offset + panel_width].set(solved)
        right_side = jnp.where(lax.axis_index("row") == root_row, placed, right_side)
    return (kernel, right_side)


def solution(mesh):
    placed = (P("row", None), P(), P(None, None, "col"), P(None, "col"), P(None, "col"), P("row"))
    return jax.shard_map(
        on_device,
        mesh=mesh,
        in_specs=placed,
        out_specs=(P("row", "col"), P("row")),
        check_vma=False,
    )
```

profile of v0, /device:TPU:0, one launch (start us, length us, event | category | flops | bytes accessed | tf_op | source)
XLA Modules:
  0.0 969.1 jit_solution(3831402307478594253)
XLA Ops:
  13.9 12.5 %divide_multiply_fusion.1 = f32[1024,512]{0,1:T(8,128)S(1)} fusion(f32[2,1024,512]{2,1,0:T(8,128)} %param.19, f32[1024,1024]{0,1:T(8,128)} %get-tuple-element.136, f32[1024]{0:T(1024)S(1)} %add_rsqrt_fusion, f32[512]{0:T(512)S(1)} %bitcast.291, f32[512]{0:T(512)S(1)} %bitcast.290), kind=kOutput, calls=%fused_computation.20 | convolution fusion | flops 6446120960 | bytes 8396800 | tf_op jit(solution)/shard_map/dot_general | solution.py:34
  35.6 13.7 %all-reduce.3 = (f32[1024]{0:T(1024)S(1)}, f32[512,1]{0,1:T(1,128)S(1)}) all-reduce(f32[1024]{0:T(1024)S(1)} %fusion.4, f32[512,1]{0,1:T(1,128)S(1)} %bitcast.282), channel_id=1, replica_groups=mesh['row'=4,'col'=8] {'row'}, use_global_device_ids=true, to_apply=%region_2.0 | all-reduce | flops 1536 | bytes 12288 | tf_op jit(solution)/shard_map/psum | solution.py:53
  54.1 147.2 %all-gather.5.cloned.1.call-done = bf16[4096,1024]{0,1:T(8,128)(2,1)} async-done(((bf16[1024,1024]{0,1:T(8,128)(2,1)}), bf16[4096,1024]{0,1:T(8,128)(2,1)}) %all-gather.5.cloned.1.call-update) | async-done | bytes 8388624 | tf_op jit(solution)/shard_map/all_gather | solution.py:58
  214.2 126.8 %all-to-all-done = bf16[8,512,1024]{1,2,0:T(8,128)(2,1)} async-done(((bf16[8,512,1024]{1,2,0:T(8,128)(2,1)}), bf16[8,512,1024]{1,2,0:T(8,128)(2,1)}, u32[]{:S(2)}, u32[]{:S(2)}) %all-to-all-start) | async-done | bytes 8388640 | tf_op jit(solution)/shard_map/all_to_all | solution.py:59
  341.0 32.8 %all-gather.3.cloned.1.call-done = bf16[1024,8192]{0,1:T(8,128)(2,1)} async-done(((bf16[1024,1024]{0,1:T(8,128)(2,1)}), bf16[1024,8192]{0,1:T(8,128)(2,1)}) %all-gather.3.cloned.1.call-update) | async-done | bytes 16777232 | tf_op jit(solution)/shard_map/all_gather | solution.py:57
  373.8 15.9 %broadcast_select_fusion.1 = (f32[1024,512]{0,1:T(8,128)}, f32[1024,512]{0,1:T(8,128)S(1)}) fusion(pred[]{:T(512)S(6)} %eq.56, s32[512]{0:T(512)S(1)} %iota_add_fusion.1, s32[1024]{0:T(1024)S(1)} %iota_add_fusion, bf16[1024,8192]{0,1:T(8,128)(2,1)} %all-gather.3.cloned.1.call-done, bf16[512,8192]{0,1:T(8,128)(2,1)} %bitcast.7), kind=kOutput, calls=%fused_computation.118 | convolution fusion | flops 8592031744 | bytes 29366272 | tf_op jit(solution)/shard_map/dot_general | solution.py:60
  392.2 51.6 %all-reduce.9.cloned.1.call-done = f32[512,512]{0,1:T(8,128)} async-done(((f32[512,512]{0,1:T(8,128)}), f32[512,512]{0,1:T(8,128)}) %all-reduce.9.cloned.1.call-update) | async-done | bytes 1048592 | tf_op jit(solution)/shard_map/psum | solution.py:13
  446.6 69.6 %all-reduce.15.cloned.1.call-done = (f32[1024,512]{0,1:T(8,128)}, f32[512,512]{0,1:T(8,128)}) async-done(((f32[1024,512]{0,1:T(8,128)}, f32[512,512]{0,1:T(8,128)}), (f32[1024,512]{0,1:T(8,128)}, f32[512,512]{0,1:T(8,128)})) %all-reduce.15.cloned.1.call-update) | async-done | bytes 3145744 | tf_op jit(solution)/shard_map/psum | solution.py:13
  519.1 11.7 %cholesky.286 = f32[128,128]{1,0:T(8,128)S(1)} custom-call(f32[128,128]{1,0:T(8,128)S(1)} %cholesky.426), custom_call_target="Cholesky" | custom-call | tf_op jit(solution)/shard_map/jit(cholesky)/cholesky | solution.py:81
  531.0 9.8 %custom-call.35 = f32[1,128,128]{1,2,0:T(8,128)S(1)} custom-call(f32[1,128,128]{2,1,0:T(8,128)S(1)} %get-tuple-element.130), custom_call_target="InvertDiagBlocksLowerTriangular" | custom-call | tf_op jit(solution)/shard_map/jit(cholesky)/cholesky | solution.py:81
  543.3 11.7 %cholesky.305 = f32[128,128]{1,0:T(8,128)S(1)} custom-call(f32[128,128]{1,0:T(8,128)S(1)} %cholesky.430), custom_call_target="Cholesky" | custom-call | tf_op jit(solution)/shard_map/jit(cholesky)/cholesky | solution.py:81
  555.1 10.0 %custom-call.36 = f32[1,128,128]{1,2,0:T(8,128)S(1)} custom-call(f32[1,128,128]{2,1,0:T(8,128)S(1)} %get-tuple-element.127), custom_call_target="InvertDiagBlocksLowerTriangular" | custom-call | tf_op jit(solution)/shard_map/jit(cholesky)/cholesky | solution.py:81
  566.6 11.7 %cholesky.326 = f32[128,128]{1,0:T(8,128)S(1)} custom-call(f32[128,128]{1,0:T(8,128)S(1)} %cholesky.435), custom_call_target="Cholesky" | custom-call | tf_op jit(solution)/shard_map/jit(cholesky)/cholesky | solution.py:81
  590.3 11.7 %cholesky.343 = f32[128,128]{1,0:T(8,128)S(1)} custom-call(f32[128,128]{1,0:T(8,128)S(1)} %convolution_subtract_fusion.17), custom_call_target="Cholesky" | custom-call | tf_op jit(solution)/shard_map/jit(cholesky)/cholesky | solution.py:81
  614.7 39.3 %custom-call.38 = f32[4,128,128]{1,2,0:T(8,128)S(1)} custom-call(f32[4,128,128]{2,1,0:T(8,128)S(1)} %get-tuple-element.72), custom_call_target="InvertDiagBlocksLowerTriangular" | custom-call | tf_op jit(solution)/shard_map/triangular_solve/custom-call.3 | solution.py:82
  676.3 51.5 %all-reduce.11.cloned.1.call-done = f32[512,512]{0,1:T(8,128)} async-done(((f32[512,512]{0,1:T(8,128)}), f32[512,512]{0,1:T(8,128)}) %all-reduce.11.cloned.1.call-update) | async-done | bytes 1048592 | tf_op jit(solution)/shard_map/psum | solution.py:13
  731.1 10.1 %psum.71 = f32[512,1]{0,1:T(1,128)S(1)} all-reduce(f32[512,1]{0,1:T(1,128)S(1)} %bitcast.285), channel_id=1, replica_groups=mesh['row'=4,'col'=8] {'row'}, use_global_device_ids=true, to_apply=%region_18.23 | all-reduce | flops 512 | bytes 4096 | tf_op jit(solution)/shard_map/psum | solution.py:13
  741.3 58.9 %all-reduce.13.cloned.1.call-done = (f32[1024,512]{0,1:T(8,128)}, f32[512,512]{0,1:T(8,128)}) async-done(((f32[1024,512]{0,1:T(8,128)}, f32[512,512]{0,1:T(8,128)}), (f32[1024,512]{0,1:T(8,128)}, f32[512,512]{0,1:T(8,128)})) %all-reduce.13.cloned.1.call-update) | async-done | bytes 3145744 | tf_op jit(solution)/shard_map/psum | solution.py:13
  803.1 11.7 %cholesky.358 = f32[128,128]{1,0:T(8,128)S(1)} custom-call(f32[128,128]{1,0:T(8,128)S(1)} %cholesky.439), custom_call_target="Cholesky" | custom-call | tf_op jit(solution)/shard_map/jit(cholesky)/cholesky | solution.py:81
  827.3 11.7 %cholesky.377 = f32[128,128]{1,0:T(8,128)S(1)} custom-call(f32[128,128]{1,0:T(8,128)S(1)} %cholesky.443), custom_call_target="Cholesky" | custom-call | tf_op jit(solution)/shard_map/jit(cholesky)/cholesky | solution.py:81
  840.4 10.2 %custom-call.41 = f32[1,128,128]{1,2,0:T(8,128)S(1)} custom-call(f32[1,128,128]{2,1,0:T(8,128)S(1)} %get-tuple-element.117), custom_call_target="InvertDiagBlocksLowerTriangular" | custom-call | tf_op jit(solution)/shard_map/jit(cholesky)/cholesky | solution.py:81
  852.2 11.7 %cholesky.398 = f32[128,128]{1,0:T(8,128)S(1)} custom-call(f32[128,128]{1,0:T(8,128)S(1)} %cholesky.448), custom_call_target="Cholesky" | custom-call | tf_op jit(solution)/shard_map/jit(cholesky)/cholesky | solution.py:81
  875.9 11.7 %cholesky.415 = f32[128,128]{1,0:T(8,128)S(1)} custom-call(f32[128,128]{1,0:T(8,128)S(1)} %convolution_subtract_fusion.16), custom_call_target="Cholesky" | custom-call | tf_op jit(solution)/shard_map/jit(cholesky)/cholesky | solution.py:81
  899.3 39.3 %custom-call.43 = f32[4,128,128]{1,2,0:T(8,128)S(1)} custom-call(f32[4,128,128]{2,1,0:T(8,128)S(1)} %get-tuple-element.74), custom_call_target="InvertDiagBlocksLowerTriangular" | custom-call | tf_op jit(solution)/shard_map/triangular_solve/custom-call.3 | solution.py:82
  (204 shorter events, 171.6 us)
Async XLA Ops:
  7.2 1.6 copy-start
  7.2 194.1 %all-gather.5.cloned.1.call-start = ((), (), s32[]{:S(2)}) async-start(), calls=%async_computation.2 | async-start | bytes 10485760 | tf_op jit(solution)/shard_map/all_gather | solution.py:58
  8.7 5.1 copy-start.19
  8.7 5.1 copy-start.20
  13.8 12.6 %copy-start.21 = (f32[2,1024,512]{2,1,0:T(8,128)S(1)}, f32[2,1024,512]{2,1,0:T(8,128)}, u32[]{:S(2)}) copy-start(f32[2,1024,512]{2,1,0:T(8,128)} %param.19) | copy-start | bytes 12582916
  13.9 12.6 %copy-start.22 = (f32[1024,1024]{0,1:T(8,128)S(1)}, f32[1024,1024]{0,1:T(8,128)}, u32[]{:S(2)}) copy-start(f32[1024,1024]{0,1:T(8,128)} %get-tuple-element.136) | copy-start | bytes 12582916
  26.4 7.2 copy-start.4
  53.3 320.5 %all-gather.3.cloned.1.call-start = ((), (), s32[]{:S(2)}) async-start(), calls=%async_computation.1 | async-start | bytes 18874368 | tf_op jit(solution)/shard_map/all_gather | solution.py:57
  209.1 131.9 %all-to-all-start = ((bf16[8,512,1024]{1,2,0:T(8,128)(2,1)}), bf16[8,512,1024]{1,2,0:T(8,128)(2,1)}, u32[]{:S(2)}, u32[]{:S(2)}) async-start(bf16[8,512,1024]{1,2,0:T(8,128)(2,1)} %bitcast.258), calls=%async_computation | async-start | bytes 16777216 | tf_op jit(solution)/shard_map/all_to_all | solution.py:59
  214.1 229.6 %all-reduce.9.cloned.1.call-start = ((), (), s32[]{:S(2)}) async-start(), calls=%async_computation.3 | async-start | bytes 2097152 | tf_op jit(solution)/shard_map/psum | solution.py:13
  389.7 1.4 copy-start.6
  392.2 124.1 %all-reduce.15.cloned.1.call-start = ((), (), s32[]{:S(2)}) async-start(), calls=%async_computation.6 | async-start | bytes 6291456 | tf_op jit(solution)/shard_map/psum | solution.py:13
  446.1 281.7 %all-reduce.11.cloned.1.call-start = ((), (), s32[]{:S(2)}) async-start(), calls=%async_computation.4 | async-start | bytes 2097152 | tf_op jit(solution)/shard_map/psum | solution.py:13
  516.2 1.7 copy-start.9
  660.3 2.9 copy-start.11
  663.3 4.8 copy-start.14
  664.3 3.7 copy-start.7
  673.2 1.4 copy-start.2
  675.7 124.5 %all-reduce.13.cloned.1.call-start = ((), (), s32[]{:S(2)}) async-start(), calls=%async_computation.5 | async-start | bytes 6291456 | tf_op jit(solution)/shard_map/psum | solution.py:13
  800.2 1.7 copy-start.8
  939.4 4.7 copy-start.16
  946.6 1.8 copy-start.10
  949.5 3.8 copy-start.3
  953.3 8.7 copy-start.1
  (6 other events, 5.6 us)
Sparse Core Ops, SparseCore 0:
  53.5 147.7 all-gather.4
  203.1 170.6 all-gather.2
  392.3 51.4 all-reduce.8
  447.6 68.6 all-reduce.14
  675.8 51.9 all-reduce.10
  731.6 68.6 all-reduce.12
where the time goes:
time: 975 us; the launch traced here: 969 us
  waiting for transfers between devices  539 us (55%)
  other arithmetic  249 us (26%)
  matrix products  92.9 us (10%)
  local copies, waits for them, and re-layouts  37.6 us (4%)
  blocking collectives  23.8 us (2%)
  between operations  20.4 us (2%)
    psum x4, waiting for transfers between devices, broadcast(): return lax.psum(block, axis)  232 us
    another operation x29, other arithmetic, on_device(): factor = jnp.linalg.cholesky(diag_block)  158 us
    all_gather x1, waiting for transfers between devices, on_device(): every_sample = lax.all_gather(centered, 'row', axis=0, tiled=True)  147 us
    all_to_all x1, waiting for transfers between devices, on_device(): lax.all_to_all(every_sample, 'col', split_axis=0, concat_axis=1, tiled=True)  127 us
    another operation x5, other arithmetic, on_device(): lax.linalg.triangular_solve(factor, column, left_side=False, lower=True,...  79.4 us
    all_gather x1, waiting for transfers between devices, on_device(): own_rows = lax.all_gather(centered, 'col', axis=1, tiled=True)  32.8 us
    dot_general x2, matrix products, jacobian(): jnp.dot(embedded, weights[panel_index], precision=lax.Precision.HIGHEST,...  19.7 us
  transfers between devices with their start and end apart: 7, of which 7 were waited for; matrix products, arithmetic and copies ran while one was open for 1% of the time, Pallas kernels for 0%

commit v1 on v0

--- a/solution.py
+++ b/solution.py
@@ -55,7 +55,12 @@
         jnp.bfloat16
     )
     own_rows = lax.all_gather(centered, "col", axis=1, tiled=True)
-    every_sample = lax.all_gather(centered, "row", axis=0, tiled=True)
+    ring = [centered]
+    for hop in range(3):
+        ring.append(lax.ppermute(ring[-1], "row", [(dev, (dev + 1) % 4) for dev in range(4)]))
+    every_sample = jnp.roll(
+        jnp.concatenate(ring[::-1], axis=0), (lax.axis_index("row") + 1) * ring[0].shape[0], axis=0
+    )
     partner = lax.all_to_all(every_sample, "col", split_axis=0, concat_axis=1, tiled=True)
     kernel = lax.dot_general(
         own_rows, partner, (((1,), (1,)), ((), ())), preferred_element_type=jnp.float32

time: 975 us -> 943 us (0.967)
  waiting for transfers between devices: 539 us -> 462 us
  local copies, waits for them, and re-layouts: 37.6 us -> 82 us
    all_gather x1 -> x0, waiting for transfers between devices: 147 us -> none  [on_device(): every_sample = lax.all_gather(centered, 'row', axis=0, tiled=True)]
    ppermute x0 -> x3, waiting for transfers between devices: none -> 139 us  [on_device(): lax.ppermute(ring[-1], 'row', [(dev, (dev + 1) % 4) for dev in range(4)])]
    all_gather x1, waiting for transfers between devices: 32.8 us -> 0.01 us  [on_device(): own_rows = lax.all_gather(centered, 'col', axis=1, tiled=True)]
    all_to_all x1, waiting for transfers between devices: 127 us -> 94 us  [on_device(): lax.all_to_all(every_sample, 'col', split_axis=0, concat_axis=1, tiled=True)]
    dynamic_slice x0 -> x2, local copies, waits for them, and re-layouts: none -> 19.7 us  [on_device(): jnp.roll(jnp.concatenate(ring[::-1], axis=0), (lax.axis_index('row') + 1)...]
    unnamed x47 -> x60, local copies, waits for them, and re-layouts: 10.2 us -> 29.4 us
  transfers between devices with their start and end apart: 7 -> 9, of which waited for: 7 -> 8; matrix products, arithmetic and copies ran while one was open for 1% -> 6% of each run, Pallas kernels for 0% -> 0%
where the time goes in v1:
time: 943 us; the launch traced here: 936 us
  waiting for transfers between devices  462 us (49%)
  other arithmetic  249 us (26%)
  matrix products  93.4 us (10%)
  local copies, waits for them, and re-layouts  82 us (9%)
  blocking collectives  23.8 us (3%)
  between operations  20.2 us (2%)
    psum x4, waiting for transfers between devices, broadcast(): return lax.psum(block, axis)  229 us
    another operation x29, other arithmetic, on_device(): factor = jnp.linalg.cholesky(diag_block)  158 us
    ppermute x3, waiting for transfers between devices, on_device(): lax.ppermute(ring[-1], 'row', [(dev, (dev + 1) % 4) for dev in range(4)])  139 us
    all_to_all x1, waiting for transfers between devices, on_device(): lax.all_to_all(every_sample, 'col', split_axis=0, concat_axis=1, tiled=True)  94 us
    another operation x5, other arithmetic, on_device(): lax.linalg.triangular_solve(factor, column, left_side=False, lower=True,...  79.2 us
    unnamed x60, local copies, waits for them, and re-layouts  29.4 us
    dot_general x2, matrix products, jacobian(): jnp.dot(embedded, weights[panel_index], precision=lax.Precision.HIGHEST,...  19.9 us
    dynamic_slice x2, local copies, waits for them, and re-layouts, on_device(): jnp.roll(jnp.concatenate(ring[::-1], axis=0), (lax.axis_index('row') + 1)...  19.7 us
  transfers between devices with their start and end apart: 9, of which 8 were waited for; matrix products, arithmetic and copies ran while one was open for 6% of the time, Pallas kernels for 0%

profile of v1, /device:TPU:0, one launch (start us, length us, event | category | flops | bytes accessed | tf_op | source)
XLA Modules:
  0.0 936.0 jit_solution(12710126732552718005)
XLA Ops:
  13.9 12.8 %divide_multiply_fusion.1 = f32[1024,512]{0,1:T(8,128)S(1)} fusion(f32[2,1024,512]{2,1,0:T(8,128)} %param.19, f32[1024,1024]{0,1:T(8,128)} %get-tuple-element.138, f32[1024]{0:T(1024)S(1)} %add_rsqrt_fusion, f32[512]{0:T(512)S(1)} %bitcast.287, f32[512]{0:T(512)S(1)} %bitcast.286), kind=kOutput, calls=%fused_computation.19 | convolution fusion | flops 6446120960 | bytes 8396800 | tf_op jit(solution)/shard_map/dot_general | solution.py:34
  35.9 13.7 %all-reduce.3 = (f32[1024]{0:T(1024)S(1)}, f32[512,1]{0,1:T(1,128)S(1)}) all-reduce(f32[1024]{0:T(1024)S(1)} %fusion.4, f32[512,1]{0,1:T(1,128)S(1)} %bitcast.278), channel_id=1, replica_groups=mesh['row'=4,'col'=8] {'row'}, use_global_device_ids=true, to_apply=%region_2.0 | all-reduce | flops 1536 | bytes 12288 | tf_op jit(solution)/shard_map/psum | solution.py:53
  53.7 47.2 %collective-permute-done = bf16[1024,1024]{0,1:T(8,128)(2,1)S(1)} collective-permute-done((bf16[1024,1024]{0,1:T(8,128)(2,1)}, bf16[1024,1024]{0,1:T(8,128)(2,1)S(1)}, u32[]{:S(2)}, u32[]{:S(2)}) %collective-permute-start) | collective-permute-done | bytes 2097184 | tf_op jit(solution)/shard_map/ppermute | solution.py:60
  102.2 46.2 %collective-permute-done.1 = bf16[1024,1024]{0,1:T(8,128)(2,1)} collective-permute-done((bf16[1024,1024]{0,1:T(8,128)(2,1)S(1)}, bf16[1024,1024]{0,1:T(8,128)(2,1)}, u32[]{:S(2)}, u32[]{:S(2)}) %collective-permute-start.1) | collective-permute-done | bytes 2097184 | tf_op jit(solution)/shard_map/ppermute | solution.py:60
  148.4 45.6 %collective-permute-done.2 = bf16[1024,1024]{0,1:T(8,128)(2,1)} collective-permute-done((bf16[1024,1024]{0,1:T(8,128)(2,1)}, bf16[1024,1024]{0,1:T(8,128)(2,1)}, u32[]{:S(2)}, u32[]{:S(2)}) %collective-permute-start.2) | collective-permute-done | bytes 2097184 | tf_op jit(solution)/shard_map/ppermute | solution.py:60
  221.1 12.0 %copy.20 = bf16[4096,1024]{1,0:T(8,128)(2,1)} copy(bf16[4096,1024]{0,1:T(8,128)(2,1)} %constant_dynamic-slice_fusion.2) | data formatting | bytes 16777216 | tf_op jit(solution)/shard_map/jit(_roll_dynamic)/dynamic_slice | solution.py:61
  238.2 94.0 %all-to-all-done = bf16[8,512,1024]{2,1,0:T(8,128)(2,1)} async-done(((bf16[8,512,1024]{2,1,0:T(8,128)(2,1)}), bf16[8,512,1024]{2,1,0:T(8,128)(2,1)}, u32[]{:S(2)}, u32[]{:S(2)}) %all-to-all-start) | async-done | bytes 8388640 | tf_op jit(solution)/shard_map/all_to_all | solution.py:64
  332.2 11.6 %copy.21 = bf16[512,8,1024]{0,2,1:T(8,128)(2,1)} copy(bf16[512,8,1024]{2,0,1:T(8,128)(2,1)} %bitcast.7) | data formatting | bytes 16777216 | tf_op jit(solution)/shard_map/all_to_all | solution.py:64
  343.8 15.9 %broadcast_select_fusion.1 = (f32[1024,512]{0,1:T(8,128)}, f32[1024,512]{0,1:T(8,128)S(1)}) fusion(pred[]{:T(512)S(6)} %eq.59, s32[512]{0:T(512)S(1)} %iota_add_fusion.1, s32[1024]{0:T(1024)S(1)} %iota_add_fusion, bf16[1024,8192]{0,1:T(8,128)(2,1)} %all-gather.2.cloned.1.call-done, bf16[512,8192]{0,1:T(8,128)(2,1)} %bitcast.263), kind=kOutput, calls=%fused_computation.117 | convolution fusion | flops 8592031744 | bytes 29366272 | tf_op jit(solution)/shard_map/dot_general | solution.py:65
  362.1 48.4 %all-reduce.9.cloned.1.call-done = f32[512,512]{0,1:T(8,128)} async-done(((f32[512,512]{0,1:T(8,128)}), f32[512,512]{0,1:T(8,128)}) %all-reduce.9.cloned.1.call-update) | async-done | bytes 1048592 | tf_op jit(solution)/shard_map/psum | solution.py:13
  412.9 70.2 %all-reduce.15.cloned.1.call-done = (f32[1024,512]{0,1:T(8,128)}, f32[512,512]{0,1:T(8,128)}) async-done(((f32[1024,512]{0,1:T(8,128)}, f32[512,512]{0,1:T(8,128)}), (f32[1024,512]{0,1:T(8,128)}, f32[512,512]{0,1:T(8,128)})) %all-reduce.15.cloned.1.call-update) | async-done | bytes 3145744 | tf_op jit(solution)/shard_map/psum | solution.py:13
  486.0 11.7 %cholesky.286 = f32[128,128]{1,0:T(8,128)S(1)} custom-call(f32[128,128]{1,0:T(8,128)S(1)} %cholesky.426), custom_call_target="Cholesky" | custom-call | tf_op jit(solution)/shard_map/jit(cholesky)/cholesky | solution.py:86
  510.2 11.7 %cholesky.305 = f32[128,128]{1,0:T(8,128)S(1)} custom-call(f32[128,128]{1,0:T(8,128)S(1)} %cholesky.430), custom_call_target="Cholesky" | custom-call | tf_op jit(solution)/shard_map/jit(cholesky)/cholesky | solution.py:86
  522.0 10.2 %custom-call.36 = f32[1,128,128]{1,2,0:T(8,128)S(1)} custom-call(f32[1,128,128]{2,1,0:T(8,128)S(1)} %get-tuple-element.129), custom_call_target="InvertDiagBlocksLowerTriangular" | custom-call | tf_op jit(solution)/shard_map/jit(cholesky)/cholesky | solution.py:86
  533.7 11.7 %cholesky.326 = f32[128,128]{1,0:T(8,128)S(1)} custom-call(f32[128,128]{1,0:T(8,128)S(1)} %cholesky.435), custom_call_target="Cholesky" | custom-call | tf_op jit(solution)/shard_map/jit(cholesky)/cholesky | solution.py:86
  557.4 11.7 %cholesky.343 = f32[128,128]{1,0:T(8,128)S(1)} custom-call(f32[128,128]{1,0:T(8,128)S(1)} %convolution_subtract_fusion.17), custom_call_target="Cholesky" | custom-call | tf_op jit(solution)/shard_map/jit(cholesky)/cholesky | solution.py:86
  581.6 39.3 %custom-call.38 = f32[4,128,128]{1,2,0:T(8,128)S(1)} custom-call(f32[4,128,128]{2,1,0:T(8,128)S(1)} %get-tuple-element.72), custom_call_target="InvertDiagBlocksLowerTriangular" | custom-call | tf_op jit(solution)/shard_map/triangular_solve/custom-call.3 | solution.py:87
  643.5 51.5 %all-reduce.11.cloned.1.call-done = f32[512,512]{0,1:T(8,128)} async-done(((f32[512,512]{0,1:T(8,128)}), f32[512,512]{0,1:T(8,128)}) %all-reduce.11.cloned.1.call-update) | async-done | bytes 1048592 | tf_op jit(solution)/shard_map/psum | solution.py:13
  708.5 58.9 %all-reduce.13.cloned.1.call-done = (f32[1024,512]{0,1:T(8,128)}, f32[512,512]{0,1:T(8,128)}) async-done(((f32[1024,512]{0,1:T(8,128)}, f32[512,512]{0,1:T(8,128)}), (f32[1024,512]{0,1:T(8,128)}, f32[512,512]{0,1:T(8,128)})) %all-reduce.13.cloned.1.call-update) | async-done | bytes 3145744 | tf_op jit(solution)/shard_map/psum | solution.py:13
  770.3 11.7 %cholesky.358 = f32[128,128]{1,0:T(8,128)S(1)} custom-call(f32[128,128]{1,0:T(8,128)S(1)} %cholesky.439), custom_call_target="Cholesky" | custom-call | tf_op jit(solution)/shard_map/jit(cholesky)/cholesky | solution.py:86
  794.5 11.7 %cholesky.377 = f32[128,128]{1,0:T(8,128)S(1)} custom-call(f32[128,128]{1,0:T(8,128)S(1)} %cholesky.443), custom_call_target="Cholesky" | custom-call | tf_op jit(solution)/shard_map/jit(cholesky)/cholesky | solution.py:86
  819.2 11.7 %cholesky.398 = f32[128,128]{1,0:T(8,128)S(1)} custom-call(f32[128,128]{1,0:T(8,128)S(1)} %cholesky.448), custom_call_target="Cholesky" | custom-call | tf_op jit(solution)/shard_map/jit(cholesky)/cholesky | solution.py:86
  842.8 11.7 %cholesky.415 = f32[128,128]{1,0:T(8,128)S(1)} custom-call(f32[128,128]{1,0:T(8,128)S(1)} %convolution_subtract_fusion.16), custom_call_target="Cholesky" | custom-call | tf_op jit(solution)/shard_map/jit(cholesky)/cholesky | solution.py:86
  866.4 39.3 %custom-call.43 = f32[4,128,128]{1,2,0:T(8,128)S(1)} custom-call(f32[4,128,128]{2,1,0:T(8,128)S(1)} %get-tuple-element.74), custom_call_target="InvertDiagBlocksLowerTriangular" | custom-call | tf_op jit(solution)/shard_map/triangular_solve/custom-call.3 | solution.py:87
  (223 shorter events, 221.7 us)
Async XLA Ops:
  7.2 336.6 %all-gather.2.cloned.1.call-start = ((), (), s32[]{:S(2)}) async-start(), calls=%async_computation.1 | async-start | bytes 18874368 | tf_op jit(solution)/shard_map/all_gather | solution.py:57
  8.7 5.1 copy-start.22
  8.7 5.1 copy-start.23
  13.8 12.8 %copy-start.24 = (f32[2,1024,512]{2,1,0:T(8,128)S(1)}, f32[2,1024,512]{2,1,0:T(8,128)}, u32[]{:S(2)}) copy-start(f32[2,1024,512]{2,1,0:T(8,128)} %param.19) | copy-start | bytes 12582916
  13.9 12.8 %copy-start.25 = (f32[1024,1024]{0,1:T(8,128)S(1)}, f32[1024,1024]{0,1:T(8,128)}, u32[]{:S(2)}) copy-start(f32[1024,1024]{0,1:T(8,128)} %get-tuple-element.138) | copy-start | bytes 12582916
  26.6 7.2 copy-start.7
  53.6 47.3 %collective-permute-start = (bf16[1024,1024]{0,1:T(8,128)(2,1)}, bf16[1024,1024]{0,1:T(8,128)(2,1)S(1)}, u32[]{:S(2)}, u32[]{:S(2)}) collective-permute-start(bf16[1024,1024]{0,1:T(8,128)(2,1)} %multiply_convert_fusion), channel_id=1, source_target_pairs={{0,8},{8,16},{16,24},{24,0},{1,9},{9,17},{17,25},{25,1},{2,10},{10... | collective-permute-start | bytes 6291464 | tf_op jit(solution)/shard_map/ppermute | solution.py:60
  102.2 46.2 %collective-permute-start.1 = (bf16[1024,1024]{0,1:T(8,128)(2,1)S(1)}, bf16[1024,1024]{0,1:T(8,128)(2,1)}, u32[]{:S(2)}, u32[]{:S(2)}) collective-permute-start(bf16[1024,1024]{0,1:T(8,128)(2,1)S(1)} %collective-permute-done), channel_id=1, source_target_pairs={{0,8},{8,16},{16,24},{24,0},{1,9},{9,17},{17,25},{25,1},{2,10},{10... | collective-permute-start | bytes 6291464 | tf_op jit(solution)/shard_map/ppermute | solution.py:60
  148.4 45.6 %collective-permute-start.2 = (bf16[1024,1024]{0,1:T(8,128)(2,1)}, bf16[1024,1024]{0,1:T(8,128)(2,1)}, u32[]{:S(2)}, u32[]{:S(2)}) collective-permute-start(bf16[1024,1024]{0,1:T(8,128)(2,1)} %collective-permute-done.1), channel_id=1, source_target_pairs={{0,8},{8,16},{16,24},{24,0},{1,9},{9,17},{17,25},{25,1},{2,10},{10... | collective-permute-start | bytes 6291464 | tf_op jit(solution)/shard_map/ppermute | solution.py:60
  197.2 3.2 copy-start.6
  200.4 2.3 copy-start.2
  233.1 99.1 %all-to-all-start = ((bf16[8,512,1024]{2,1,0:T(8,128)(2,1)}), bf16[8,512,1024]{2,1,0:T(8,128)(2,1)}, u32[]{:S(2)}, u32[]{:S(2)}) async-start(bf16[8,512,1024]{2,1,0:T(8,128)(2,1)} %bitcast.254), calls=%async_computation | async-start | bytes 16777216 | tf_op jit(solution)/shard_map/all_to_all | solution.py:64
  238.2 172.4 %all-reduce.9.cloned.1.call-start = ((), (), s32[]{:S(2)}) async-start(), calls=%async_computation.2 | async-start | bytes 2097152 | tf_op jit(solution)/shard_map/psum | solution.py:13
  362.1 121.0 %all-reduce.15.cloned.1.call-start = ((), (), s32[]{:S(2)}) async-start(), calls=%async_computation.5 | async-start | bytes 6291456 | tf_op jit(solution)/shard_map/psum | solution.py:13
  412.8 282.1 %all-reduce.11.cloned.1.call-start = ((), (), s32[]{:S(2)}) async-start(), calls=%async_computation.3 | async-start | bytes 2097152 | tf_op jit(solution)/shard_map/psum | solution.py:13
  483.1 1.7 copy-start.12
  627.3 2.9 copy-start.14
  630.2 4.8 copy-start.17
  631.3 3.8 copy-start.10
  642.9 124.5 %all-reduce.13.cloned.1.call-start = ((), (), s32[]{:S(2)}) async-start(), calls=%async_computation.4 | async-start | bytes 6291456 | tf_op jit(solution)/shard_map/psum | solution.py:13
  906.4 4.7 copy-start.19
  913.6 1.8 copy-start.13
  916.5 3.8 copy-start.4
  920.3 8.8 copy-start.1
  (11 other events, 12.8 us)
Sparse Core Ops, SparseCore 0:
  53.7 87.9 all-gather.1
  362.2 48.2 all-reduce.8
  414.4 68.6 all-reduce.14
  643.0 51.9 all-reduce.10
  698.7 68.6 all-reduce.12
